TPU v7x, 256 devices: a whole 4x4x8 slice. The times are simulated.
256 devices in a mesh: mirror: 2 (over y_hi), slab: 64 (over z, y_lo, x), cols: 2 (over core).
Axes of the slice: x: 4, y: 4 (y_hi: 2, y_lo: 2; y = y_hi * 2 + y_lo), z: 8, core: 2. Of those that a mesh axis runs over, the one named last changes fastest.
Arguments:
- right_side: float32 [2, 1024, 65536], P('mirror', 'slab', 'cols'), parts along dimension 2, may hold values from -6 to 6
- analysis: float32 [2, 1024, 1024], P('mirror'), may hold values from -0.1875 to 0.1875
- synthesis: float32 [2, 1024, 1024], P('mirror'), may hold values from -0.1875 to 0.1875
- negated_eigen: float32 [2, 1024], P('mirror'), may hold values from 0.25 to 4
- wave_square: float32 [65536], P(('cols', 'slab')), parts along dimension 0, may hold values from 0.25 to 4
Outputs:
- solution: float32 [2, 1024, 65536], P('mirror', 'slab', 'cols'), parts along dimension 2
There are 2 independent parts, one for each index of `cols`. A program takes and returns all parts, laid end to end along the dimension named above; an argument that names none is the same for every part. Nothing has to cross between parts.
All inputs are finite; a program needn't handle non-finite values.
Results may differ from a plain program's by a relative error of at most 0.0001.
Values sent between devices are 32-bit elements; how exact they have to be, the bound alone decides.
No kernel may reach another device: no remote copies, remote signals or barrier semaphores. Data moves between devices by JAX's collectives and lax.ppermute only.
A program may use at most 64 MiB of HBM per device.

v0:
```python
import jax
import jax.numpy as jnp
from jax import lax
from jax.sharding import PartitionSpec as P


def from_partner(value, axis, bit):
    mask = 2**bit
    pairs = [(source, source ^ mask) for source in range(lax.axis_size(axis))]
    return lax.ppermute(value, axis, pairs)


def mirror_swap(slab_piece):
    return from_partner(slab_piece, "mirror", 0)


def project(column_field, analysis, synthesis, negated_eigen, wave_square):
    coefficients = jnp.dot(
        analysis, column_field, precision=lax.Precision.HIGHEST, preferred_element_type=jnp.float32
    )
    scaled = coefficients / (negated_eigen[:, None] + wave_square[None, :])
    return -jnp.dot(
        synthesis, scaled, precision=lax.Precision.HIGHEST, preferred_element_type=jnp.float32
    )


def shards(right_side, analysis, synthesis, negated_eigen, wave_square):
    own_half = right_side[0]
    parity = lax.axis_index("mirror")
    parity_sign = (1 - 2 * parity).astype(jnp.float32)
    partner = mirror_swap(own_half)
    lower_half = jnp.where(parity == 0, own_half, partner)
    upper_half = jnp.where(parity == 0, partner, own_half)
    folded = (lower_half + parity_sign * upper_half) * 0.5
    columns = lax.all_to_all(folded, "slab", split_axis=1, concat_axis=0, tiled=True)
    solved = project(columns, analysis[0], synthesis[0], negated_eigen[0], wave_square)
    returned = lax.all_to_all(solved, "slab", split_axis=0, concat_axis=1, tiled=True)
    partner_back = mirror_swap(returned)
    even_part = jnp.where(parity == 0, returned, partner_back)
    odd_part = jnp.where(parity == 0, partner_back, returned)
    result = even_part + parity_sign * odd_part
    return result[None]


def solution(mesh):
    return jax.shard_map(
        shards,
        mesh=mesh,
        in_specs=(
            P("mirror", "slab", "cols"),
            P("mirror", None, None),
            P("mirror", None, None),
            P("mirror", None),
            P(("cols", "slab")),
        ),
        out_specs=P("mirror", "slab", "cols"),
        check_vma=False,
    )
```

profile of v0, /device:TPU:36, one launch (start us, length us, event | category | flops | bytes accessed | tf_op | source)
XLA Modules:
  0.0 242.4 jit_solution(17822131640532167315)
XLA Ops:
  0.0 3.2 %collective-permute-start = (f32[16,32768]{1,0:T(8,128)}, f32[16,32768]{1,0:T(8,128)S(1)}, u32[]{:S(2)}, u32[]{:S(2)}) collective-permute-start(f32[16,32768]{1,0:T(8,128)} %bitcast.39), channel_id=1, source_target_pairs={{0,128},{128,0},{1,129},{129,1},{2,130},{130,2},{3,131},{131,3},{4... | collective-permute-start | bytes 6291464 | tf_op jit(solution)/shard_map/ppermute | solution.py:10
  3.2 45.9 %collective-permute-done = f32[16,32768]{1,0:T(8,128)S(1)} collective-permute-done((f32[16,32768]{1,0:T(8,128)}, f32[16,32768]{1,0:T(8,128)S(1)}, u32[]{:S(2)}, u32[]{:S(2)}) %collective-permute-start) | collective-permute-done | bytes 2097184 | tf_op jit(solution)/shard_map/ppermute | solution.py:10
  49.1 1.9 add_multiply_fusion
  51.0 0.2 copy.17
  51.2 0.0 copy-start
  51.3 61.3 %all_to_all.38 = f32[16,64,512]{2,0,1:T(8,128)S(1)} all-to-all(f32[16,64,512]{2,0,1:T(8,128)S(1)} %bitcast.36), channel_id=1, replica_groups=mesh['mirror'=2,'slab'=64,'cols'=2] {'slab'}, dimensions={1} | all-to-all | bytes 4194304 | tf_op jit(solution)/shard_map/all_to_all | solution.py:35
  112.6 0.0 copy-done
  112.6 0.0 copy-start.1
  112.6 0.0 copy-start.2
  112.6 0.0 copy-start.3
  112.6 13.6 %fusion.2 = f32[512,1024]{1,0:T(8,128)S(1)} fusion(f32[1024,512]{1,0:T(8,128)S(1)} %bitcast.32, f32[1,1024,1024]{2,1,0:T(8,128)S(1)} %copy-done), kind=kOutput, calls=%fused_computation.2 | convolution fusion | flops 6442450944 | bytes 8388608 | tf_op jit(solution)/shard_map/dot_general | solution.py:18
  126.2 0.0 copy-done.1
  126.2 0.0 copy-done.2
  126.2 0.0 copy-done.3
  126.2 8.4 %negate_bitcast_fusion = f32[1024,512]{0,1:T(8,128)} fusion(f32[1,1024,1024]{2,1,0:T(8,128)S(1)} %copy-done.1, f32[512,1024]{1,0:T(8,128)S(1)} %fusion.2, f32[512]{0:T(512)S(1)} %copy-done.3, f32[1024]{0:T(1024)S(1)} %bitcast.40), kind=kOutput, calls=%fused_computation.7 | convolution fusion | flops 6444023808 | bytes 8394752 | tf_op jit(solution)/shard_map/dot_general | solution.py:22
  134.6 1.9 copy.12
  136.6 56.0 %all_to_all.39 = f32[64,16,512]{2,1,0:T(8,128)S(1)} all-to-all(f32[64,16,512]{2,1,0:T(8,128)S(1)} %bitcast.37), channel_id=1, replica_groups=mesh['mirror'=2,'slab'=64,'cols'=2] {'slab'}, dimensions={0} | all-to-all | bytes 4194304 | tf_op jit(solution)/shard_map/all_to_all | solution.py:37
  192.5 0.2 copy.15
  192.7 3.0 %collective-permute-start.1 = (f32[16,32768]{1,0:T(8,128)S(1)}, f32[16,32768]{1,0:T(8,128)S(1)}, u32[]{:S(2)}, u32[]{:S(2)}) collective-permute-start(f32[16,32768]{1,0:T(8,128)S(1)} %bitcast.33), channel_id=1, source_target_pairs={{0,128},{128,0},{1,129},{129,1},{2,130},{130,2},{3,131},{131,3},{4... | collective-permute-start | bytes 6291464 | tf_op jit(solution)/shard_map/ppermute | solution.py:10
  195.7 45.2 %collective-permute-done.1 = f32[16,32768]{1,0:T(8,128)S(1)} collective-permute-done((f32[16,32768]{1,0:T(8,128)S(1)}, f32[16,32768]{1,0:T(8,128)S(1)}, u32[]{:S(2)}, u32[]{:S(2)}) %collective-permute-start.1) | collective-permute-done | bytes 2097184 | tf_op jit(solution)/shard_map/ppermute | solution.py:10
  240.8 1.6 add_bitcast_fusion
Async XLA Ops:
  0.0 49.1 %collective-permute-start = (f32[16,32768]{1,0:T(8,128)}, f32[16,32768]{1,0:T(8,128)S(1)}, u32[]{:S(2)}, u32[]{:S(2)}) collective-permute-start(f32[16,32768]{1,0:T(8,128)} %bitcast.39), channel_id=1, source_target_pairs={{0,128},{128,0},{1,129},{129,1},{2,130},{130,2},{3,131},{131,3},{4... | collective-permute-start | bytes 6291464 | tf_op jit(solution)/shard_map/ppermute | solution.py:10
  51.2 61.3 %copy-start = (f32[1,1024,1024]{2,1,0:T(8,128)S(1)}, f32[1,1024,1024]{2,1,0:T(8,128)}, u32[]{:S(2)}) copy-start(f32[1,1024,1024]{2,1,0:T(8,128)} %param.6) | copy-start | bytes 12582916
  112.6 13.7 %copy-start.1 = (f32[1,1024,1024]{2,1,0:T(8,128)S(1)}, f32[1,1024,1024]{2,1,0:T(8,128)}, u32[]{:S(2)}) copy-start(f32[1,1024,1024]{2,1,0:T(8,128)} %param.7) | copy-start | bytes 12582916
  112.6 13.7 %copy-start.2 = (f32[1,1024]{1,0:T(1,128)S(1)}, f32[1,1024]{1,0:T(1,128)}, u32[]{:S(2)}) copy-start(f32[1,1024]{1,0:T(1,128)} %param.8) | copy-start | bytes 12292
  112.6 13.7 %copy-start.3 = (f32[512]{0:T(512)S(1)}, f32[512]{0:T(512)}, u32[]{:S(2)}) copy-start(f32[512]{0:T(512)} %param.9) | copy-start | bytes 6148
  192.7 48.1 %collective-permute-start.1 = (f32[16,32768]{1,0:T(8,128)S(1)}, f32[16,32768]{1,0:T(8,128)S(1)}, u32[]{:S(2)}, u32[]{:S(2)}) collective-permute-start(f32[16,32768]{1,0:T(8,128)S(1)} %bitcast.33), channel_id=1, source_target_pairs={{0,128},{128,0},{1,129},{129,1},{2,130},{130,2},{3,131},{131,3},{4... | collective-permute-start | bytes 6291464 | tf_op jit(solution)/shard_map/ppermute | solution.py:10
where the time goes:
time: 243 us; the launch traced here: 242 us
  blocking collectives  117 us (48%)
  waiting for transfers between devices  91 us (37%)
  matrix products  22 us (9%)
  starting transfers between devices  6.18 us (3%)
  other arithmetic  3.53 us (1%)
    ppermute x2, waiting for transfers between devices, from_partner(): return lax.ppermute(value, axis, pairs)  91 us
    all_to_all x1, blocking collectives, shards(): lax.all_to_all(folded, 'slab', split_axis=1, concat_axis=0, tiled=True)  61.3 us
    all_to_all x1, blocking collectives, shards(): lax.all_to_all(solved, 'slab', split_axis=0, concat_axis=1, tiled=True)  56 us
    dot_general x1, matrix products, project(): jnp.dot(analysis, column_field, precision=lax.Precision.HIGHEST, preferre...  13.6 us
    dot_general x1, matrix products, project(): jnp.dot(synthesis, scaled, precision=lax.Precision.HIGHEST, preferred_ele...  8.39 us
    ppermute x2, starting transfers between devices, from_partner(): return lax.ppermute(value, axis, pairs)  6.18 us
  transfers between devices with their start and end apart: 2, of which 2 were waited for; matrix products, arithmetic and copies ran while one was open for 0% of the time, Pallas kernels for 0%

commit v1 on v0

--- a/solution.py
+++ b/solution.py
@@ -34,7 +34,10 @@
     folded = (lower_half + parity_sign * upper_half) * 0.5
     columns = lax.all_to_all(folded, "slab", split_axis=1, concat_axis=0, tiled=True)
     solved = project(columns, analysis[0], synthesis[0], negated_eigen[0], wave_square)
-    returned = lax.all_to_all(solved, "slab", split_axis=0, concat_axis=1, tiled=True)
+    returned = jnp.concatenate(
+        lax.all_to_all(jnp.stack(jnp.split(solved, lax.axis_size("slab"), axis=0)), "slab", 0, 0),
+        axis=1,
+    )
     partner_back = mirror_swap(returned)
     even_part = jnp.where(parity == 0, returned, partner_back)
     odd_part = jnp.where(parity == 0, partner_back, returned)

time: 243 us -> 366 us (1.51)
  local copies, waits for them, and re-layouts: 2.33 us -> 123 us
    another operation x0 -> x69, local copies, waits for them, and re-layouts: none -> 102 us  [shards(): jnp.stack(jnp.split(solved, lax.axis_size('slab'), axis=0))]
    unnamed x8 -> x137, local copies, waits for them, and re-layouts: 0.02 us -> 20.1 us
where the time goes in v1:
time: 366 us; the launch traced here: 362 us
  local copies, waits for them, and re-layouts  123 us (34%)
  blocking collectives  117 us (32%)
  waiting for transfers between devices  91 us (25%)
  matrix products  20.6 us (6%)
  starting transfers between devices  6.18 us (2%)
    another operation x69, local copies, waits for them, and re-layouts, shards(): jnp.stack(jnp.split(solved, lax.axis_size('slab'), axis=0))  102 us
    ppermute x2, waiting for transfers between devices, from_partner(): return lax.ppermute(value, axis, pairs)  91 us
    all_to_all x1, blocking collectives, shards(): lax.all_to_all(folded, 'slab', split_axis=1, concat_axis=0, tiled=True)  61.3 us
    all_to_all x1, blocking collectives, shards(): lax.all_to_all(jnp.stack(jnp.split(solved, lax.axis_size('slab'), axis=0)...  56 us
    unnamed x137, local copies, waits for them, and re-layouts  20.1 us
    dot_general x1, matrix products, project(): jnp.dot(analysis, column_field, precision=lax.Precision.HIGHEST, preferre...  13.5 us
  transfers between devices with their start and end apart: 2, of which 2 were waited for; matrix products, arithmetic and copies ran while one was open for 0% of the time, Pallas kernels for 0%

profile of v1, /device:TPU:36, one launch (start us, length us, event | category | flops | bytes accessed | tf_op | source)
XLA Modules:
  0.0 362.3 jit_solution(9721545643774538609)
XLA Ops:
  0.0 3.2 collective-permute-start
  3.2 45.9 %collective-permute-done = f32[16,32768]{1,0:T(8,128)S(1)} collective-permute-done((f32[16,32768]{1,0:T(8,128)}, f32[16,32768]{1,0:T(8,128)S(1)}, u32[]{:S(2)}, u32[]{:S(2)}) %collective-permute-start) | collective-permute-done | bytes 2097184 | tf_op jit(solution)/shard_map/ppermute | solution.py:10
  49.1 1.9 add_multiply_fusion
  51.3 61.3 %all_to_all.24 = f32[16,64,512]{2,0,1:T(8,128)S(1)} all-to-all(f32[16,64,512]{2,0,1:T(8,128)S(1)} %bitcast.163), channel_id=1, replica_groups=mesh['mirror'=2,'slab'=64,'cols'=2] {'slab'}, dimensions={1} | all-to-all | bytes 4194304 | tf_op jit(solution)/shard_map/all_to_all | solution.py:35
  112.6 13.5 %fusion.2 = f32[512,1024]{1,0:T(8,128)S(1)} fusion(f32[1024,512]{1,0:T(8,128)S(1)} %bitcast.159, f32[1,1024,1024]{2,1,0:T(8,128)S(1)} %copy-done), kind=kOutput, calls=%fused_computation.2 | convolution fusion | flops 6442450944 | bytes 8388608 | tf_op jit(solution)/shard_map/dot_general | solution.py:18
  126.1 7.1 %negate_bitcast_fusion = f32[1024,512]{0,1:T(8,128)S(1)} fusion(f32[1,1024,1024]{2,1,0:T(8,128)S(1)} %copy-done.34, f32[512,1024]{1,0:T(8,128)S(1)} %fusion.2, f32[512]{0:T(512)S(1)} %copy-done.36, f32[1024]{0:T(1024)S(1)} %bitcast.166), kind=kOutput, calls=%fused_computation.7 | convolution fusion | flops 6444023808 | bytes 8394752 | tf_op jit(solution)/shard_map/dot_general | solution.py:22
  133.6 3.4 slice_bitcast_fusion.38
  137.0 3.4 slice_bitcast_fusion
  140.4 3.0 slice_bitcast_fusion.19
  147.8 1.7 copy.107
  149.5 1.7 copy.106
  151.2 1.7 copy.105
  152.8 1.7 copy.104
  154.5 1.7 copy.103
  156.2 1.7 copy.102
  157.8 1.7 copy.101
  159.5 1.7 copy.100
  161.2 1.7 copy.99
  162.8 1.7 copy.98
  164.5 1.7 copy.97
  166.2 1.7 copy.96
  167.8 1.7 copy.95
  169.5 1.7 copy.94
  171.2 1.7 copy.93
  172.8 1.7 copy.92
  174.5 1.7 copy.91
  176.2 1.7 copy.90
  177.8 1.7 copy.89
  180.5 1.1 copy.144
  181.6 1.1 copy.143
  182.6 1.1 copy.142
  183.7 1.7 copy.141
  185.4 1.7 copy.140
  187.0 1.7 copy.139
  188.7 1.7 copy.138
  190.4 1.7 copy.137
  192.0 1.7 copy.136
  193.7 1.7 copy.135
  195.4 1.7 copy.134
  197.1 1.7 copy.133
  198.7 1.7 copy.132
  200.4 1.7 copy.131
  202.1 1.7 copy.130
  203.7 1.7 copy.129
  205.4 1.7 copy.128
  207.0 1.7 copy.127
  208.7 1.7 copy.126
  210.4 1.7 copy.125
  212.0 1.7 copy.124
  213.7 1.7 copy.123
  215.4 1.7 copy.122
  217.0 1.7 copy.121
  218.7 1.7 copy.120
  220.4 1.7 copy.119
  222.0 1.7 copy.118
  223.7 1.7 copy.117
  225.4 1.7 copy.116
  227.0 1.7 copy.115
  228.7 1.7 copy.114
  230.4 1.7 copy.113
  256.4 56.0 %all_to_all.25 = f32[64,16,512]{2,1,0:T(8,128)S(1)} all-to-all(f32[64,16,512]{2,1,0:T(8,128)S(1)} %constant_dynamic-update-slice_fusion), channel_id=1, replica_groups=mesh['mirror'=2,'slab'=64,'cols'=2] {'slab'}, dimensions={0} | all-to-all | bytes 4194304 | tf_op jit(solution)/shard_map/all_to_all | solution.py:38
  312.5 3.0 collective-permute-start.1
  315.5 45.2 %collective-permute-done.1 = f32[16,32768]{1,0:T(8,128)S(1)} collective-permute-done((f32[16,32768]{1,0:T(8,128)S(1)}, f32[16,32768]{1,0:T(8,128)S(1)}, u32[]{:S(2)}, u32[]{:S(2)}) %collective-permute-start.1) | collective-permute-done | bytes 2097184 | tf_op jit(solution)/shard_map/ppermute | solution.py:10
  360.7 1.6 add_bitcast_fusion
  (154 shorter events, 30.0 us)
Async XLA Ops:
  0.0 49.1 %collective-permute-start = (f32[16,32768]{1,0:T(8,128)}, f32[16,32768]{1,0:T(8,128)S(1)}, u32[]{:S(2)}, u32[]{:S(2)}) collective-permute-start(f32[16,32768]{1,0:T(8,128)} %bitcast.165), channel_id=1, source_target_pairs={{0,128},{128,0},{1,129},{129,1},{2,130},{130,2},{3,131},{131,3},{4... | collective-permute-start | bytes 6291464 | tf_op jit(solution)/shard_map/ppermute | solution.py:10
  51.2 61.3 %copy-start = (f32[1,1024,1024]{2,1,0:T(8,128)S(1)}, f32[1,1024,1024]{2,1,0:T(8,128)}, u32[]{:S(2)}) copy-start(f32[1,1024,1024]{2,1,0:T(8,128)} %param.6) | copy-start | bytes 12582916
  112.6 13.5 %copy-start.34 = (f32[1,1024,1024]{2,1,0:T(8,128)S(1)}, f32[1,1024,1024]{2,1,0:T(8,128)}, u32[]{:S(2)}) copy-start(f32[1,1024,1024]{2,1,0:T(8,128)} %param.7) | copy-start | bytes 12582916
  112.6 13.5 %copy-start.35 = (f32[1,1024]{1,0:T(1,128)S(1)}, f32[1,1024]{1,0:T(1,128)}, u32[]{:S(2)}) copy-start(f32[1,1024]{1,0:T(1,128)} %param.8) | copy-start | bytes 12292
  112.6 13.5 %copy-start.36 = (f32[512]{0:T(512)S(1)}, f32[512]{0:T(512)}, u32[]{:S(2)}) copy-start(f32[512]{0:T(512)} %param.9) | copy-start | bytes 6148
  232.7 17.6 %copy-start.18 = (f32[1,16,512]{2,1,0:T(8,128)S(1)}, f32[1,16,512]{2,1,0:T(8,128)}, u32[]{:S(2)}) copy-start(f32[1,16,512]{2,1,0:T(8,128)} %copy.104) | copy-start | bytes 98308
  232.7 17.6 %copy-start.16 = (f32[1,16,512]{2,1,0:T(8,128)S(1)}, f32[1,16,512]{2,1,0:T(8,128)}, u32[]{:S(2)}) copy-start(f32[1,16,512]{2,1,0:T(8,128)} %copy.105) | copy-start | bytes 98308
  232.7 17.6 %copy-start.14 = (f32[1,16,512]{2,1,0:T(8,128)S(1)}, f32[1,16,512]{2,1,0:T(8,128)}, u32[]{:S(2)}) copy-start(f32[1,16,512]{2,1,0:T(8,128)} %copy.106) | copy-start | bytes 98308
  232.7 17.6 %copy-start.12 = (f32[1,16,512]{2,1,0:T(8,128)S(1)}, f32[1,16,512]{2,1,0:T(8,128)}, u32[]{:S(2)}) copy-start(f32[1,16,512]{2,1,0:T(8,128)} %copy.107) | copy-start | bytes 98308
  232.7 23.3 %copy-start.17 = (f32[1,16,512]{2,1,0:T(8,128)S(1)}, f32[1,16,512]{2,1,0:T(8,128)}, u32[]{:S(2)}) copy-start(f32[1,16,512]{2,1,0:T(8,128)} %copy.128) | copy-start | bytes 98308
  232.8 23.3 %copy-start.15 = (f32[1,16,512]{2,1,0:T(8,128)S(1)}, f32[1,16,512]{2,1,0:T(8,128)}, u32[]{:S(2)}) copy-start(f32[1,16,512]{2,1,0:T(8,128)} %copy.129) | copy-start | bytes 98308
  232.8 23.3 %copy-start.13 = (f32[1,16,512]{2,1,0:T(8,128)S(1)}, f32[1,16,512]{2,1,0:T(8,128)}, u32[]{:S(2)}) copy-start(f32[1,16,512]{2,1,0:T(8,128)} %copy.130) | copy-start | bytes 98308
  232.8 23.3 %copy-start.11 = (f32[1,16,512]{2,1,0:T(8,128)S(1)}, f32[1,16,512]{2,1,0:T(8,128)}, u32[]{:S(2)}) copy-start(f32[1,16,512]{2,1,0:T(8,128)} %copy.131) | copy-start | bytes 98308
  233.5 16.8 %copy-start.22 = (f32[1,16,512]{2,1,0:T(8,128)S(1)}, f32[1,16,512]{2,1,0:T(8,128)}, u32[]{:S(2)}) copy-start(f32[1,16,512]{2,1,0:T(8,128)} %copy.102) | copy-start | bytes 98308
  233.5 16.8 %copy-start.20 = (f32[1,16,512]{2,1,0:T(8,128)S(1)}, f32[1,16,512]{2,1,0:T(8,128)}, u32[]{:S(2)}) copy-start(f32[1,16,512]{2,1,0:T(8,128)} %copy.103) | copy-start | bytes 98308
  233.5 22.5 %copy-start.21 = (f32[1,16,512]{2,1,0:T(8,128)S(1)}, f32[1,16,512]{2,1,0:T(8,128)}, u32[]{:S(2)}) copy-start(f32[1,16,512]{2,1,0:T(8,128)} %copy.126) | copy-start | bytes 98308
  233.5 22.5 %copy-start.19 = (f32[1,16,512]{2,1,0:T(8,128)S(1)}, f32[1,16,512]{2,1,0:T(8,128)}, u32[]{:S(2)}) copy-start(f32[1,16,512]{2,1,0:T(8,128)} %copy.127) | copy-start | bytes 98308
  233.5 22.6 %copy-start.10 = (f32[1,16,512]{2,1,0:T(8,128)S(1)}, f32[1,16,512]{2,1,0:T(8,128)}, u32[]{:S(2)}) copy-start(f32[1,16,512]{2,1,0:T(8,128)} %copy.132) | copy-start | bytes 98308
  233.5 22.6 %copy-start.9 = (f32[1,16,512]{2,1,0:T(8,128)S(1)}, f32[1,16,512]{2,1,0:T(8,128)}, u32[]{:S(2)}) copy-start(f32[1,16,512]{2,1,0:T(8,128)} %copy.133) | copy-start | bytes 98308
  233.5 22.6 %copy-start.8 = (f32[1,16,512]{2,1,0:T(8,128)S(1)}, f32[1,16,512]{2,1,0:T(8,128)}, u32[]{:S(2)}) copy-start(f32[1,16,512]{2,1,0:T(8,128)} %copy.134) | copy-start | bytes 98308
  233.5 22.6 %copy-start.7 = (f32[1,16,512]{2,1,0:T(8,128)S(1)}, f32[1,16,512]{2,1,0:T(8,128)}, u32[]{:S(2)}) copy-start(f32[1,16,512]{2,1,0:T(8,128)} %copy.135) | copy-start | bytes 98308
  234.3 21.6 %copy-start.25 = (f32[1,16,512]{2,1,0:T(8,128)S(1)}, f32[1,16,512]{2,1,0:T(8,128)}, u32[]{:S(2)}) copy-start(f32[1,16,512]{2,1,0:T(8,128)} %copy.123) | copy-start | bytes 98308
  234.3 21.7 %copy-start.24 = (f32[1,16,512]{2,1,0:T(8,128)S(1)}, f32[1,16,512]{2,1,0:T(8,128)}, u32[]{:S(2)}) copy-start(f32[1,16,512]{2,1,0:T(8,128)} %copy.124) | copy-start | bytes 98308
  234.3 21.7 %copy-start.23 = (f32[1,16,512]{2,1,0:T(8,128)S(1)}, f32[1,16,512]{2,1,0:T(8,128)}, u32[]{:S(2)}) copy-start(f32[1,16,512]{2,1,0:T(8,128)} %copy.125) | copy-start | bytes 98308
  234.3 21.9 %copy-start.6 = (f32[1,16,512]{2,1,0:T(8,128)S(1)}, f32[1,16,512]{2,1,0:T(8,128)}, u32[]{:S(2)}) copy-start(f32[1,16,512]{2,1,0:T(8,128)} %copy.136) | copy-start | bytes 98308
  234.3 21.9 %copy-start.5 = (f32[1,16,512]{2,1,0:T(8,128)S(1)}, f32[1,16,512]{2,1,0:T(8,128)}, u32[]{:S(2)}) copy-start(f32[1,16,512]{2,1,0:T(8,128)} %copy.137) | copy-start | bytes 98308
  234.3 22.0 %copy-start.4 = (f32[1,16,512]{2,1,0:T(8,128)S(1)}, f32[1,16,512]{2,1,0:T(8,128)}, u32[]{:S(2)}) copy-start(f32[1,16,512]{2,1,0:T(8,128)} %copy.138) | copy-start | bytes 98308
  234.3 22.0 %copy-start.3 = (f32[1,16,512]{2,1,0:T(8,128)S(1)}, f32[1,16,512]{2,1,0:T(8,128)}, u32[]{:S(2)}) copy-start(f32[1,16,512]{2,1,0:T(8,128)} %copy.139) | copy-start | bytes 98308
  234.3 22.0 %copy-start.2 = (f32[1,16,512]{2,1,0:T(8,128)S(1)}, f32[1,16,512]{2,1,0:T(8,128)}, u32[]{:S(2)}) copy-start(f32[1,16,512]{2,1,0:T(8,128)} %copy.140) | copy-start | bytes 98308
  235.0 20.7 %copy-start.32 = (f32[1,16,512]{2,1,0:T(8,128)S(1)}, f32[1,16,512]{2,1,0:T(8,128)}, u32[]{:S(2)}) copy-start(f32[1,16,512]{2,1,0:T(8,128)} %copy.116) | copy-start | bytes 98308
  235.0 20.7 %copy-start.31 = (f32[1,16,512]{2,1,0:T(8,128)S(1)}, f32[1,16,512]{2,1,0:T(8,128)}, u32[]{:S(2)}) copy-start(f32[1,16,512]{2,1,0:T(8,128)} %copy.117) | copy-start | bytes 98308
  235.0 20.7 %copy-start.30 = (f32[1,16,512]{2,1,0:T(8,128)S(1)}, f32[1,16,512]{2,1,0:T(8,128)}, u32[]{:S(2)}) copy-start(f32[1,16,512]{2,1,0:T(8,128)} %copy.118) | copy-start | bytes 98308
  235.0 20.8 %copy-start.29 = (f32[1,16,512]{2,1,0:T(8,128)S(1)}, f32[1,16,512]{2,1,0:T(8,128)}, u32[]{:S(2)}) copy-start(f32[1,16,512]{2,1,0:T(8,128)} %copy.119) | copy-start | bytes 98308
  235.0 20.8 %copy-start.28 = (f32[1,16,512]{2,1,0:T(8,128)S(1)}, f32[1,16,512]{2,1,0:T(8,128)}, u32[]{:S(2)}) copy-start(f32[1,16,512]{2,1,0:T(8,128)} %copy.120) | copy-start | bytes 98308
  235.1 20.8 %copy-start.27 = (f32[1,16,512]{2,1,0:T(8,128)S(1)}, f32[1,16,512]{2,1,0:T(8,128)}, u32[]{:S(2)}) copy-start(f32[1,16,512]{2,1,0:T(8,128)} %copy.121) | copy-start | bytes 98308
  235.1 20.8 %copy-start.26 = (f32[1,16,512]{2,1,0:T(8,128)S(1)}, f32[1,16,512]{2,1,0:T(8,128)}, u32[]{:S(2)}) copy-start(f32[1,16,512]{2,1,0:T(8,128)} %copy.122) | copy-start | bytes 98308
  235.1 21.2 %copy-start.1 = (f32[1,16,512]{2,1,0:T(8,128)S(1)}, f32[1,16,512]{2,1,0:T(8,128)}, u32[]{:S(2)}) copy-start(f32[1,16,512]{2,1,0:T(8,128)} %copy.141) | copy-start | bytes 98308
  235.8 19.9 %copy-start.33 = (f32[1,16,512]{2,1,0:T(8,128)S(1)}, f32[1,16,512]{2,1,0:T(8,128)}, u32[]{:S(2)}) copy-start(f32[1,16,512]{2,1,0:T(8,128)} %copy.115) | copy-start | bytes 98308
  312.5 48.1 %collective-permute-start.1 = (f32[16,32768]{1,0:T(8,128)S(1)}, f32[16,32768]{1,0:T(8,128)S(1)}, u32[]{:S(2)}, u32[]{:S(2)}) collective-permute-start(f32[16,32768]{1,0:T(8,128)S(1)} %bitcast.160), channel_id=1, source_target_pairs={{0,128},{128,0},{1,129},{129,1},{2,130},{130,2},{3,131},{131,3},{4... | collective-permute-start | bytes 6291464 | tf_op jit(solution)/shard_map/ppermute | solution.py:10
